TPU v7x, 1024 devices: a whole 4x4x32 slice. The times are simulated.
1024 devices in a mesh: group: 32 (over y, x, core), shuf: 32 (over z).
Axes of the slice: x: 4, y: 4, z: 32, core: 2. Of those that a mesh axis runs over, the one named last changes fastest.
Arguments:
- inputs: bfloat16 [32, 8192, 512], P('group', 'shuf'), may hold values from -8 to 8
- cotangent: bfloat16 [32, 8192, 512], P('group', 'shuf'), may hold values from -8 to 8
- w_uvqk: bfloat16 [512, 2048], P('group'), may hold values from -0.25 to 0.25
- w_out: bfloat16 [512, 512], P('group'), may hold values from -0.25 to 0.25
- send_perm: int32 [32, 32, 32], P('group', 'shuf'), may hold values from 0 to 31, each once within a row
- recv_perm: int32 [32, 32, 32], P('group', 'shuf'), may hold values from 0 to 31, each once within a row
- lengths: int32 [32, 32, 8], P('group', 'shuf'), may hold values from 1 to 128, 256 in all within a row
- prefixes: int32 [32, 32, 8], P('group', 'shuf'), may hold values from 0 to 32
Outputs:
- layer_out: bfloat16 [32, 8192, 512], P('group', 'shuf')
- grad_input: bfloat16 [32, 8192, 512], P('group', 'shuf')
- grad_uvqk: float32 [512, 2048], P('group')
- grad_wout: float32 [512, 512], P('group')
All inputs are finite; a program needn't handle non-finite values.
Results may differ from a plain program's by a relative error of at most 0.03.
Values may be sent and summed in bfloat16 or wider, within the bound.
A program may use at most 32 MiB of HBM per device.

v0:
```python
from functools import partial

import jax
import jax.numpy as jnp
from jax import lax
from jax.sharding import PartitionSpec as P

D = 512
HEADS = 8
ROWS = 256


norm_eps = 1e-05


def normalize(values):
    center = jnp.mean(values, axis=-1, keepdims=True)
    centred = values - center
    variance = jnp.mean(centred * centred, axis=-1, keepdims=True)
    inv_scale = lax.rsqrt(variance + norm_eps)
    return (centred * inv_scale, inv_scale)


def silu_slope(values):
    sigma = jax.nn.sigmoid(values)
    return sigma * (1.0 + values * (1.0 - sigma))


def visible(user_lengths, user_prefixes, row_count):
    user_ends = jnp.cumsum(user_lengths)
    row_index = jnp.arange(row_count, dtype=jnp.int32)
    user_index = jnp.sum((row_index[:, None] >= user_ends[None, :]).astype(jnp.int32), axis=1)
    member = user_index[:, None] == jnp.arange(user_lengths.shape[0], dtype=jnp.int32)[None, :]
    starts = user_ends - user_lengths
    position = row_index - jnp.sum(jnp.where(member, starts[None, :], 0), axis=1)
    prefix_len = jnp.sum(jnp.where(member, user_prefixes[None, :], 0), axis=1)
    same_user = user_index[:, None] == user_index[None, :]
    return same_user & (
        (row_index[None, :] <= row_index[:, None]) | (position[None, :] < prefix_len[:, None])
    )


def attention(activated, weight_out, residual, allowed):
    row_count = activated.shape[0]
    gate_u = activated[:, :D]
    values = activated[:, D : 2 * D].reshape(row_count, HEADS, D // HEADS)
    queries = activated[:, 2 * D : 3 * D].reshape(row_count, HEADS, D // HEADS)
    keys = activated[:, 3 * D :].reshape(row_count, HEADS, D // HEADS)
    scores = jnp.einsum("qhd,khd->hqk", queries, keys, preferred_element_type=jnp.float32)
    weights = (jnp.where(allowed[None], jax.nn.silu(scores), 0.0) / ROWS).astype(jnp.bfloat16)
    mixed = jnp.einsum("hqk,khd->qhd", weights, values, preferred_element_type=jnp.float32).reshape(
        row_count, D
    )
    normed, unused = normalize(mixed)
    gated = (normed * gate_u.astype(jnp.float32)).astype(jnp.bfloat16)
    return (jnp.dot(gated, weight_out, preferred_element_type=jnp.float32) + residual).astype(
        jnp.bfloat16
    )


def on_device(inputs, cotangent, w_uvqk, w_out, send_perm, recv_perm, lengths, prefixes):
    row_count = inputs.shape[1]
    feature_width = inputs.shape[2]
    send_order = send_perm[0, 0]
    recv_order = recv_perm[0, 0]
    blocks = send_order.shape[0]
    block_rows = row_count // blocks

    def regroup(array, order):
        return jnp.take(array.reshape(blocks, block_rows, feature_width), order, axis=0).reshape(
            row_count, feature_width
        )

    def inverse(order):
        return jnp.zeros_like(order).at[order].set(jnp.arange(blocks, dtype=jnp.int32))

    full_uvqk, full_out = (
        lax.all_gather(w_uvqk, "group", axis=0, tiled=True),
        lax.all_gather(w_out, "group", axis=0, tiled=True),
    )
    outgoing = (regroup(inputs[0], send_order), regroup(cotangent[0], send_order))
    arrived = (
        lax.all_to_all(outgoing[0], "shuf", split_axis=0, concat_axis=0, tiled=True),
        lax.all_to_all(outgoing[1], "shuf", split_axis=0, concat_axis=0, tiled=True),
    )
    local_x = regroup(arrived[0], recv_order)
    local_cot = regroup(arrived[1], recv_order)
    inputs_f32 = local_x.astype(jnp.float32)
    centred, inv_scale = normalize(inputs_f32)
    normed_x = centred.astype(jnp.bfloat16)
    projected = jnp.dot(normed_x, full_uvqk, preferred_element_type=jnp.float32)
    activated = jax.nn.silu(projected).astype(jnp.bfloat16)
    allowed = visible(lengths[0, 0], prefixes[0, 0], row_count)
    layer_value, pullback = jax.vjp(
        partial(attention, allowed=allowed), activated, full_out, inputs_f32
    )
    grad_act, grad_weight, grad_res = pullback(local_cot)
    grad_proj = (grad_act.astype(jnp.float32) * silu_slope(projected)).astype(jnp.bfloat16)
    grad_normed = lax.dot_general(
        grad_proj, full_uvqk, (((1,), (1,)), ((), ())), preferred_element_type=jnp.float32
    )
    grad_center = jnp.mean(grad_normed, axis=-1, keepdims=True)
    grad_proj_z = jnp.mean(grad_normed * centred, axis=-1, keepdims=True)
    grad_rows = (inv_scale * (grad_normed - grad_center - centred * grad_proj_z) + grad_res).astype(
        jnp.bfloat16
    )
    recv_back = inverse(recv_order)
    returned = (
        lax.all_to_all(
            regroup(layer_value, recv_back), "shuf", split_axis=0, concat_axis=0, tiled=True
        ),
        lax.all_to_all(
            regroup(grad_rows, recv_back), "shuf", split_axis=0, concat_axis=0, tiled=True
        ),
    )
    send_back = inverse(send_order)
    owner_out = regroup(returned[0], send_back)[None]
    owner_grad = regroup(returned[1], send_back)[None]
    part_uvqk = lax.dot_general(
        normed_x, grad_proj, (((0,), (0,)), ((), ())), preferred_element_type=jnp.float32
    )
    part_proj, part_out = (
        lax.psum_scatter(
            part_uvqk.astype(jnp.bfloat16), "group", scatter_dimension=0, tiled=True
        ).astype(jnp.float32),
        lax.psum_scatter(
            grad_weight.astype(jnp.float32).astype(jnp.bfloat16),
            "group",
            scatter_dimension=0,
            tiled=True,
        ).astype(jnp.float32),
    )
    grad_uvqk, grad_wout = (
        lax.psum(part_proj.astype(jnp.bfloat16), "shuf").astype(jnp.float32),
        lax.psum(part_out.astype(jnp.bfloat16), "shuf").astype(jnp.float32),
    )
    return (owner_out, owner_grad, grad_uvqk, grad_wout)


def solution(mesh):
    return jax.shard_map(
        on_device,
        mesh=mesh,
        in_specs=(
            P("group", "shuf", None),
            P("group", "shuf", None),
            P("group", None),
            P("group", None),
            P("group", "shuf", None),
            P("group", "shuf", None),
            P("group", "shuf", None),
            P("group", "shuf", None),
        ),
        out_specs=(
            P("group", "shuf", None),
            P("group", "shuf", None),
            P("group", None),
            P("group", None),
        ),
        check_vma=False,
    )
```

profile of v0, /device:TPU:6, one launch (start us, length us, event | category | flops | bytes accessed | tf_op | source)
XLA Modules:
  0.0 713.4 jit_solution(3779934328627774364)
XLA Ops:
  7.2 0.7 compare_select_fusion.3
  7.9 0.7 compare_and_fusion.3
  8.6 0.6 gather_fusion.4
  9.2 1.5 gather_fusion
  10.7 0.9 broadcast_select_fusion.4
  11.6 28.7 %all-to-all-start = ((bf16[32,8,512]{2,1,0:T(8,128)(2,1)}), bf16[32,8,512]{2,1,0:T(8,128)(2,1)S(1)}, u32[]{:S(2)}, u32[]{:S(2)}) async-start(bf16[32,8,512]{2,1,0:T(8,128)(2,1)} %get-tuple-element.23), calls=%async_computation | async-start | bytes 524288 | tf_op jit(solution)/shard_map/all_to_all | solution.py:83
  40.4 0.7 all-gather.2.cloned.1.call-update
  41.1 0.2 reduce-window.7
  41.3 0.7 scatter_custom_fusion
  42.1 40.8 %all-to-all-done = bf16[32,8,512]{2,1,0:T(8,128)(2,1)S(1)} async-done(((bf16[32,8,512]{2,1,0:T(8,128)(2,1)}), bf16[32,8,512]{2,1,0:T(8,128)(2,1)S(1)}, u32[]{:S(2)}, u32[]{:S(2)}) %all-to-all-start) | async-done | bytes 262176 | tf_op jit(solution)/shard_map/all_to_all | solution.py:83
  82.9 3.9 all-to-all-start.2
  86.8 0.1 select_reduce_fusion
  86.8 24.8 %all_gather.7 = bf16[512,512]{1,0:T(8,128)(2,1)S(1)} all-gather(bf16[16,512]{1,0:T(8,128)(2,1)S(1)} %copy-done.9), channel_id=1, replica_groups=mesh['group'=32,'shuf'=32] {'group'}, dimensions={0}, use_global_device_ids=true | all-gather | bytes 540672 | tf_op jit(solution)/shard_map/all_gather | solution.py:79
  111.7 0.1 fusion.24
  111.8 0.6 gather_fusion.1
  112.4 0.2 convert_reduce_fusion
  112.6 0.1 div.48
  112.7 0.2 fusion.17
  112.9 0.1 rsqrt.22
  113.0 14.7 %all-to-all-done.2 = bf16[32,8,512]{2,1,0:T(8,128)(2,1)S(1)} async-done(((bf16[32,8,512]{2,1,0:T(8,128)(2,1)}), bf16[32,8,512]{2,1,0:T(8,128)(2,1)S(1)}, u32[]{:S(2)}, u32[]{:S(2)}) %all-to-all-start.2) | async-done | bytes 262176 | tf_op jit(solution)/shard_map/all_to_all | solution.py:84
  127.7 0.6 gather_fusion.5
  128.3 3.7 multiply_convert_fusion.2
  132.0 1.0 copy-done.1
  133.1 0.1 copy.31
  133.2 0.1 copy.32
  133.4 0.1 copy.33
  133.6 2.1 multiply_convert_fusion.1
  135.6 0.5 fusion.38
  136.1 0.2 copy.34
  136.3 0.1 fusion.19
  136.4 1.4 multiply_reduce_fusion
  137.8 1.3 fusion.36
  139.2 0.1 broadcast_add_fusion
  139.3 0.8 copy.35
  140.1 2.0 fusion.39
  142.1 2.8 fusion.1
  144.9 0.4 fusion.40
  145.4 0.3 fusion.41
  145.7 0.2 copy-done.8
  145.9 0.1 copy.38
  146.0 0.1 copy.37
  146.2 0.1 copy.36
  146.3 0.3 fusion.4
  146.6 2.6 multiply_convert_fusion
  149.2 0.9 fusion.35
  150.1 0.3 fusion.20
  150.4 0.6 gather_fusion.6
  151.0 0.6 gather_fusion.2
  151.5 0.9 broadcast_select_fusion
  152.4 19.7 %all-to-all-start.3 = ((bf16[32,8,512]{2,1,0:T(8,128)(2,1)}), bf16[32,8,512]{2,1,0:T(8,128)(2,1)S(1)}, u32[]{:S(2)}, u32[]{:S(2)}) async-start(bf16[32,8,512]{2,1,0:T(8,128)(2,1)} %get-tuple-element.20), calls=%async_computation.3 | async-start | bytes 524288 | tf_op jit(solution)/shard_map/all_to_all | solution.py:112
  172.2 1.2 convolution_convert_fusion.2
  173.4 2.3 convolution_convert_fusion
  175.7 39.3 %all-to-all-done.3 = bf16[32,8,512]{2,1,0:T(8,128)(2,1)S(1)} async-done(((bf16[32,8,512]{2,1,0:T(8,128)(2,1)}), bf16[32,8,512]{2,1,0:T(8,128)(2,1)S(1)}, u32[]{:S(2)}, u32[]{:S(2)}) %all-to-all-start.3) | async-done | bytes 262176 | tf_op jit(solution)/shard_map/all_to_all | solution.py:112
  215.0 3.9 all-to-all-start.1
  218.9 0.7 scatter_custom_fusion.1
  219.7 88.9 %reduce-scatter.5.cloned.1.call-done = bf16[16,512]{1,0:T(8,128)(2,1)} async-done(((bf16[512,512]{1,0:T(8,128)(2,1)}), bf16[16,512]{1,0:T(8,128)(2,1)}) %reduce-scatter.5.cloned.1.call-update) | async-done | bytes 16400 | tf_op jit(solution)/shard_map/reduce_scatter | solution.py:126
  308.6 110.0 %psum.15 = bf16[16,512]{1,0:T(8,128)(2,1)S(1)} all-reduce(bf16[16,512]{1,0:T(8,128)(2,1)} %reduce-scatter.5.cloned.1.call-done), channel_id=1, replica_groups=mesh['group'=32,'shuf'=32] {'shuf'}, use_global_device_ids=true, to_apply=%region_17.19 | all-reduce | flops 8192 | bytes 32768 | tf_op jit(solution)/shard_map/psum | solution.py:135
  418.6 0.6 convert_element_type.122
  419.2 0.6 gather_fusion.7
  419.8 0.6 gather_fusion.3
  420.4 26.4 %reduce-scatter.3.cloned.1.call-done = bf16[16,2048]{1,0:T(8,128)(2,1)} async-done(((bf16[512,2048]{1,0:T(8,128)(2,1)}), bf16[16,2048]{1,0:T(8,128)(2,1)}) %reduce-scatter.3.cloned.1.call-update) | async-done | bytes 65552 | tf_op jit(solution)/shard_map/reduce_scatter | solution.py:123
  446.8 0.9 select_bitcast_fusion
  447.7 257.6 %all-reduce.6.cloned.1.call-done = bf16[16,2048]{1,0:T(8,128)(2,1)} async-done(((bf16[16,2048]{1,0:T(8,128)(2,1)}), bf16[16,2048]{1,0:T(8,128)(2,1)}) %all-reduce.6.cloned.1.call-update) | async-done | bytes 65552 | tf_op jit(solution)/shard_map/psum | solution.py:134
  705.3 1.5 convert_element_type.120
  (61 shorter events, 0.6 us)
Async XLA Ops:
  7.2 1.4 copy-start
  7.2 33.9 %copy-start.12 = (s32[1,1,8]{2,1,0:T(1,128)S(1)}, s32[1,1,8]{2,1,0:T(1,128)}, u32[]{:S(2)}) copy-start(s32[1,1,8]{2,1,0:T(1,128)} %param.16) | copy-start | bytes 100
  7.2 34.1 %copy-start.13 = (s32[1,1,32]{2,1,0:T(1,128)S(1)}, s32[1,1,32]{2,1,0:T(1,128)}, u32[]{:S(2)}) copy-start(s32[1,1,32]{2,1,0:T(1,128)} %param.15) | copy-start | bytes 388
  7.2 79.5 %copy-start.10 = (s32[1,1,8]{2,1,0:T(1,128)S(1)}, s32[1,1,8]{2,1,0:T(1,128)}, u32[]{:S(2)}) copy-start(s32[1,1,8]{2,1,0:T(1,128)} %param.17) | copy-start | bytes 100
  7.2 79.6 %copy-start.9 = (bf16[16,512]{1,0:T(8,128)(2,1)S(1)}, bf16[16,512]{1,0:T(8,128)(2,1)}, u32[]{:S(2)}) copy-start(bf16[16,512]{1,0:T(8,128)(2,1)} %param.13) | copy-start | bytes 49156
  11.6 71.2 %all-to-all-start = ((bf16[32,8,512]{2,1,0:T(8,128)(2,1)}), bf16[32,8,512]{2,1,0:T(8,128)(2,1)S(1)}, u32[]{:S(2)}, u32[]{:S(2)}) async-start(bf16[32,8,512]{2,1,0:T(8,128)(2,1)} %get-tuple-element.23), calls=%async_computation | async-start | bytes 524288 | tf_op jit(solution)/shard_map/all_to_all | solution.py:83
  40.3 88.0 %all-gather.2.cloned.1.call-start = ((), (), s32[]{:S(2)}) async-start(), calls=%async_computation.6 | async-start | bytes 2162688 | tf_op jit(solution)/shard_map/all_gather | solution.py:78
  82.9 44.9 %all-to-all-start.2 = ((bf16[32,8,512]{2,1,0:T(8,128)(2,1)}), bf16[32,8,512]{2,1,0:T(8,128)(2,1)S(1)}, u32[]{:S(2)}, u32[]{:S(2)}) async-start(bf16[32,8,512]{2,1,0:T(8,128)(2,1)} %get-tuple-element.22), calls=%async_computation.2 | async-start | bytes 524288 | tf_op jit(solution)/shard_map/all_to_all | solution.py:84
  132.0 1.0 copy-start.1
  133.2 2.4 copy-start.2
  133.4 2.2 copy-start.4
  133.5 2.1 copy-start.6
  139.1 2.9 copy-start.3
  142.1 2.8 copy-start.7
  142.1 3.3 copy-start.5
  144.9 1.0 copy-start.8
  146.6 2.6 copy-start.11
  152.4 62.5 %all-to-all-start.3 = ((bf16[32,8,512]{2,1,0:T(8,128)(2,1)}), bf16[32,8,512]{2,1,0:T(8,128)(2,1)S(1)}, u32[]{:S(2)}, u32[]{:S(2)}) async-start(bf16[32,8,512]{2,1,0:T(8,128)(2,1)} %get-tuple-element.20), calls=%async_computation.3 | async-start | bytes 524288 | tf_op jit(solution)/shard_map/all_to_all | solution.py:112
  172.1 136.5 %reduce-scatter.5.cloned.1.call-start = ((), (), s32[]{:S(2)}) async-start(), calls=%async_computation.9 | async-start | bytes 540672 | tf_op jit(solution)/shard_map/reduce_scatter | solution.py:126
  173.4 273.4 %reduce-scatter.3.cloned.1.call-start = ((), (), s32[]{:S(2)}) async-start(), calls=%async_computation.7 | async-start | bytes 2162688 | tf_op jit(solution)/shard_map/reduce_scatter | solution.py:123
  175.7 43.2 %copy-start.14 = (s32[1,1,32]{2,1,0:T(1,128)S(1)}, s32[1,1,32]{2,1,0:T(1,128)}, u32[]{:S(2)}) copy-start(s32[1,1,32]{2,1,0:T(1,128)} %param.14) | copy-start | bytes 388
  215.0 204.8 %all-to-all-start.1 = ((bf16[32,8,512]{2,1,0:T(8,128)(2,1)}), bf16[32,8,512]{2,1,0:T(8,128)(2,1)S(1)}, u32[]{:S(2)}, u32[]{:S(2)}) async-start(bf16[32,8,512]{2,1,0:T(8,128)(2,1)} %get-tuple-element.21), calls=%async_computation.1 | async-start | bytes 524288 | tf_op jit(solution)/shard_map/all_to_all | solution.py:109
  218.9 486.5 %all-reduce.6.cloned.1.call-start = ((), (), s32[]{:S(2)}) async-start(), calls=%async_computation.8 | async-start | bytes 131072 | tf_op jit(solution)/shard_map/psum | solution.py:134
Sparse Core Ops, SparseCore 0:
  45.5 79.4 all-gather.1
  178.4 130.1 reduce-scatter.4
  314.2 132.5 reduce-scatter.2
  449.0 256.3 all-reduce.5
where the time goes:
time: 714 us; the launch traced here: 713 us
  waiting for transfers between devices  468 us (66%)
  blocking collectives  135 us (19%)
  starting transfers between devices  56.3 us (8%)
  matrix products  17.8 us (2%)
  between operations  14.3 us (2%)
  other arithmetic  11.6 us (2%)
  local copies, waits for them, and re-layouts  10.2 us (1%)
    psum x1, waiting for transfers between devices, on_device(): lax.psum(part_proj.astype(jnp.bfloat16), 'shuf').astype(jnp.float32)  258 us
    psum x1, blocking collectives, on_device(): lax.psum(part_out.astype(jnp.bfloat16), 'shuf').astype(jnp.float32)  110 us
    reduce_scatter x1, waiting for transfers between devices, on_device(): lax.psum_scatter(grad_weight.astype(jnp.float32).astype(jnp.bfloat16), 'g...  88.9 us
    all_to_all x1, waiting for transfers between devices, on_device(): lax.all_to_all(outgoing[0], 'shuf', split_axis=0, concat_axis=0, tiled=True)  40.8 us
    all_to_all x1, waiting for transfers between devices, on_device(): lax.all_to_all(regroup(grad_rows, recv_back), 'shuf', split_axis=0, conca...  39.3 us
    all_to_all x1, starting transfers between devices, on_device(): lax.all_to_all(outgoing[0], 'shuf', split_axis=0, concat_axis=0, tiled=True)  28.7 us
    reduce_scatter x1, waiting for transfers between devices, on_device(): lax.psum_scatter(part_uvqk.astype(jnp.bfloat16), 'group', scatter_dimensi...  26.4 us
    all_gather x1, blocking collectives, on_device(): lax.all_gather(w_out, 'group', axis=0, tiled=True)  24.8 us
  transfers between devices with their start and end apart: 8, of which 6 were waited for; matrix products, arithmetic and copies ran while one was open for 1% of the time, Pallas kernels for 0%

commit v1 on v0

v1 whole, which is shorter than its diff:
```python
import jax
import jax.numpy as jnp
from jax import lax
from jax.experimental import pallas as pl
from jax.experimental.pallas import tpu as pltpu
from jax.sharding import PartitionSpec as P

D = 512
HEADS = 8
ROWS = 256
BLOCK = 8
BLK = 32
USERS = 8
NZ = 32
SEG = 8
NSEG = 4
COLS = 2560
HALF = 1280
QUART = 640
EPS = 1e-05
MESH = pl.DeviceIdType.MESH
F32 = jnp.float32
BF16 = jnp.bfloat16


def dot(a, b, ca, cb):
    return lax.dot_general(a, b, (((ca,), (cb,)), ((), ())), preferred_element_type=F32)


def kernel(
    x_in, c_in, wu_in, wo_in, sp_in, rp_in, len_in, pre_in,
    out_ref, grad_ref, gu_ref, go_ref,
    xs, xr, cs, cr, os_, or_, gs, gr,
    wfull, pb, rc, sa, sb, sa2, sb2, ta, tb, ta2, tb2, ua, ub, ua2, ub2,
    z1, r1, z2, r2, z3, r3,
    pts, ptr, vis, xf, zf, inv, xn, act, dact, mixed, gated, gproj, w8, d8,
    a2a_send, a2a_recv, ag_send, ag_recv, rs_send, rs_recv, ar_send, ar_recv,
):
    g = lax.axis_index("group")
    z = lax.axis_index("shuf")
    core = g % 2
    xx = (g // 2) % 4
    yy = g // 8

    def gid(y, x, c):
        return (y * 4 + x) * 2 + c

    xplus = (gid(yy, (xx + 1) % 4, core), z)
    xminus = (gid(yy, (xx + 3) % 4, core), z)
    yplus = (gid((yy + 1) % 4, xx, core), z)
    yminus = (gid((yy + 3) % 4, xx, core), z)
    partner = (gid(yy, xx, 1 - core), z)

    def remote(src, dst, ssem, rsem, dev):
        return pltpu.make_async_remote_copy(
            src_ref=src, dst_ref=dst, send_sem=ssem, recv_sem=rsem,
            device_id=dev, device_id_type=MESH,
        )

    barrier = pltpu.get_barrier_semaphore()
    for dev in (xplus, xminus, yplus, yminus, partner):
        pl.semaphore_signal(barrier, inc=1, device_id=dev, device_id_type=MESH)

    def greet(k, carry):
        pl.semaphore_signal(
            barrier, inc=1, device_id=(g, (z + 1 + k) % NZ), device_id_type=MESH
        )
        return carry

    lax.fori_loop(0, NZ - 1, greet, 0)

    lane = lax.broadcasted_iota(jnp.int32, (1, ROWS), 1)
    row_of = lax.broadcasted_iota(jnp.int32, (ROWS, ROWS), 0)

    def one_hot(perm_ref):
        index = lane % BLOCK
        for t in range(BLK):
            index = index + jnp.where(lane // BLOCK == t, perm_ref[t] * BLOCK, 0)
        return (row_of == index).astype(F32).astype(BF16)

    pts[...] = one_hot(sp_in)
    ptr[...] = one_hot(rp_in)

    def to_blocks(value):
        return value.reshape(BLK, BLOCK, D).astype(BF16)

    def rows_of(ref):
        return ref[...].astype(F32).reshape(ROWS, D)

    xs[...] = to_blocks(dot(pts[...], x_in[...], 0, 0))
    cs[...] = to_blocks(dot(pts[...], c_in[...], 0, 0))
    xr[z] = xs[z]
    cr[z] = cs[z]

    wfull[yy, xx, core, :, 0 : 4 * D] = wu_in[...]
    wfull[yy, xx, core, :, 4 * D : COLS] = wo_in[...]
    ri = lax.broadcasted_iota(jnp.int32, (ROWS, 1), 0)
    uid_r = jnp.zeros((ROWS, 1), jnp.int32)
    uid_k = jnp.zeros((1, ROWS), jnp.int32)
    pre_r = jnp.zeros((ROWS, 1), jnp.int32) + pre_in[0]
    start_k = jnp.zeros((1, ROWS), jnp.int32)
    end = len_in[0]
    for u in range(USERS):
        past_r = ri >= end
        past_k = lane >= end
        uid_r = uid_r + jnp.where(past_r, 1, 0)
        uid_k = uid_k + jnp.where(past_k, 1, 0)
        start_k = start_k + jnp.where(past_k, len_in[u], 0)
        if u < USERS - 1:
            pre_r = pre_r + jnp.where(past_r, pre_in[u + 1] - pre_in[u], 0)
            end = end + len_in[u + 1]
    allowed = jnp.where(
        uid_r == uid_k,
        jnp.where(lane <= ri, 1.0, jnp.where(lane - start_k < pre_r, 1.0, 0.0)),
        0.0,
    )
    vis[...] = allowed * (1.0 / ROWS)

    pl.semaphore_wait(barrier, NZ - 1 + 5)

    def exchange(which, src, dst, first, last, near):
        def step(k, carry):
            j = NZ - 2 - k if near else k
            m = (j + 1) // 2
            off = NZ // 2 + m * (2 * (j % 2) - 1)
            peer = (z + off) % NZ
            remote(
                src.at[peer], dst.at[z], a2a_send.at[which], a2a_recv.at[which], (g, peer)
            ).start()
            return carry

        lax.fori_loop(first, last, step, 0)

    def exchange_wait(which, buf, recv):
        part = buf.at[pl.ds(0, NZ - 1)]
        copy = remote(
            part, part, a2a_send.at[which], a2a_recv.at[which], (g, (z + 1) % NZ)
        )
        if recv:
            copy.wait_recv()
        else:
            copy.wait_send()

    exchange(0, xs, xr, 0, NZ - 1, True)

    own = wfull.at[yy, xx, core]
    w_x0 = remote(own, own, ag_send.at[0], ag_recv.at[0], xplus)
    w_x1 = remote(own, own, ag_send.at[1], ag_recv.at[1], xminus)
    w_x0.start()
    w_x1.start()
    exchange(1, cs, cr, 0, NZ - 1, False)

    def half_x(x, h):
        return wfull.at[yy, x, core, :, pl.ds(h * HALF, HALF)]

    w_x0.wait_recv()
    left = half_x((xx + 3) % 4, 0)
    w_x2 = remote(left, left, ag_send.at[2], ag_recv.at[2], xplus)
    w_x2.start()
    w_x1.wait_recv()
    right = half_x((xx + 1) % 4, 1)
    w_x3 = remote(right, right, ag_send.at[3], ag_recv.at[3], xminus)
    w_x3.start()
    w_x2.wait_recv()
    w_x3.wait_recv()
    mine = wfull.at[yy, :, core]
    w_y0 = remote(mine, mine, ag_send.at[4], ag_recv.at[4], yplus)
    w_y1 = remote(mine, mine, ag_send.at[5], ag_recv.at[5], yminus)
    w_y0.start()
    w_y1.start()

    def half_y(y, h):
        return wfull.at[y, pl.ds(2 * h, 2), core]

    w_y0.wait_recv()
    down = half_y((yy + 3) % 4, 0)
    w_y2 = remote(down, down, ag_send.at[6], ag_recv.at[6], yplus)
    w_y2.start()
    w_y1.wait_recv()
    up = half_y((yy + 1) % 4, 1)
    w_y3 = remote(up, up, ag_send.at[7], ag_recv.at[7], yminus)
    w_y3.start()
    w_y2.wait_recv()
    w_y3.wait_recv()
    column = wfull.at[:, :, core]
    w_c = remote(column, column, ag_send.at[8], ag_recv.at[8], partner)
    w_c.start()

    exchange_wait(0, xr, True)
    x32 = dot(ptr[...], rows_of(xr).astype(BF16), 0, 0)
    xf[...] = x32
    center = jnp.mean(x32, axis=-1, keepdims=True)
    centred = x32 - center
    scale = lax.rsqrt(jnp.mean(centred * centred, axis=-1, keepdims=True) + EPS)
    inv[...] = jnp.broadcast_to(scale, (ROWS, 128))
    normed_x = centred * scale
    zf[...] = normed_x
    xn[...] = normed_x.astype(BF16)
    w_c.wait_recv()

    def weight(c):
        return wfull[:, :, :, :, pl.ds(pl.multiple_of(c * D, D), D)].reshape(D, D)

    def project(c, carry):
        cols = pl.ds(pl.multiple_of(c * D, D), D)
        p = dot(xn[...], weight(c), 1, 0)
        s = jax.nn.sigmoid(p)
        act[:, cols] = (p * s).astype(BF16)
        dact[:, cols] = s * (1.0 + p * (1.0 - s))
        return carry

    lax.fori_loop(0, 4, project, 0)

    lane128 = lax.broadcasted_iota(jnp.int32, (ROWS, 128), 1)

    def pair_cols(base, p):
        return pl.ds(pl.multiple_of(base * D + p * 128, 128), 128)

    def attend(p, carry):
        v = act[:, pair_cols(1, p)]
        q = act[:, pair_cols(2, p)].astype(F32)
        k = act[:, pair_cols(3, p)]
        parts = []
        for h in range(2):
            inside = (lane128 // 64) == h
            qh = jnp.where(inside, q, 0.0).astype(BF16)
            scores = dot(qh, k, 1, 1)
            s = jax.nn.sigmoid(scores)
            allow = vis[...]
            wts = (scores * s * allow).astype(BF16)
            w8[2 * p + h] = wts
            d8[2 * p + h] = s * (1.0 + scores * (1.0 - s)) * allow
            parts.append(dot(wts, v, 1, 0))
        mixed[:, pl.ds(pl.multiple_of(p * 128, 128), 128)] = jnp.where(
            lane128 < 64, parts[0], parts[1]
        )
        return carry

    lax.fori_loop(0, HEADS // 2, attend, 0)

    m32 = mixed[...]
    m_center = jnp.mean(m32, axis=-1, keepdims=True)
    m_centred = m32 - m_center
    m_scale = lax.rsqrt(jnp.mean(m_centred * m_centred, axis=-1, keepdims=True) + EPS)
    m_normed = m_centred * m_scale
    mixed[...] = m_normed
    gated[...] = (m_normed * act[:, 0:D].astype(F32)).astype(BF16)
    layer = (dot(gated[...], weight(4), 1, 0) + xf[...]).astype(BF16)
    os_[...] = to_blocks(dot(ptr[...], layer, 1, 0))
    or_[z] = os_[z]
    exchange(2, os_, or_, 0, NZ - 1, False)

    exchange_wait(1, cr, True)
    cot = dot(ptr[...], rows_of(cr).astype(BF16), 0, 0)
    cot16 = cot.astype(BF16)
    xf[...] = cot
    pb[:, :, :, :, 4 * D : COLS] = (
        dot(gated[...], cot16, 0, 0).astype(BF16).reshape(4, 4, 2, 16, D)
    )
    g_gated = dot(cot16, weight(4), 1, 1).astype(BF16).astype(F32)
    m_normed = mixed[...]
    g_normed = g_gated * act[:, 0:D].astype(F32)
    g_u = (g_gated * m_normed).astype(BF16).astype(F32)
    gproj[:, 0:D] = (g_u * dact[:, 0:D]).astype(BF16)
    g_mixed = m_scale * (
        g_normed
        - jnp.mean(g_normed, axis=-1, keepdims=True)
        - m_normed * jnp.mean(g_normed * m_normed, axis=-1, keepdims=True)
    )
    gated[...] = g_mixed.astype(BF16)

    def attend_back(p, carry):
        v = act[:, pair_cols(1, p)]
        q = act[:, pair_cols(2, p)]
        k = act[:, pair_cols(3, p)]
        gm = gated[:, pl.ds(pl.multiple_of(p * 128, 128), 128)]
        gv, gq, gk = [], [], []
        for h in range(2):
            inside = (lane128 // 64) == h
            gmh = jnp.where(inside, gm.astype(F32), 0.0).astype(BF16)
            g_w = dot(gmh, v, 1, 1).astype(BF16).astype(F32)
            g_s = (g_w * d8[2 * p + h]).astype(BF16)
            gv.append(dot(w8[2 * p + h], gm, 0, 0))
            gq.append(dot(g_s, k, 1, 0))
            gk.append(dot(g_s, q, 0, 0))
        for base, part in ((1, gv), (2, gq), (3, gk)):
            value = jnp.where(lane128 < 64, part[0], part[1]).astype(BF16).astype(F32)
            cols = pair_cols(base, p)
            gproj[:, cols] = (value * dact[:, cols]).astype(BF16)
        return carry

    lax.fori_loop(0, HEADS // 2, attend_back, 0)

    def weight_grad(c, carry):
        cols = pl.ds(pl.multiple_of(c * D, D), D)
        part = dot(xn[...], gproj[:, cols], 0, 0)
        pb[:, :, :, :, cols] = part.astype(BF16).reshape(4, 4, 2, 16, D)
        return carry

    lax.fori_loop(0, 4, weight_grad, 0)

    other = pb.at[:, :, 1 - core]
    p_c = remote(other, rc, rs_send.at[0], rs_recv.at[0], partner)
    p_c.start()

    mixed[...] = dot(gproj[:, 0:D], weight(0), 1, 1)

    def input_grad(c, carry):
        cols = pl.ds(pl.multiple_of(c * D, D), D)
        mixed[...] = mixed[...] + dot(gproj[:, cols], weight(c), 1, 1)
        return carry

    lax.fori_loop(1, 4, input_grad, 0)
    g_xn = mixed[...]
    zz = zf[...]
    g_x = inv[:, 0:1] * (
        g_xn
        - jnp.mean(g_xn, axis=-1, keepdims=True)
        - zz * jnp.mean(g_xn * zz, axis=-1, keepdims=True)
    ) + xf[...]
    gs[...] = to_blocks(dot(ptr[...], g_x.astype(BF16), 1, 0))
    gr[z] = gs[z]
    exchange(3, gs, gr, 0, 8, False)

    p_c.wait_recv()

    def core_sum(i, carry):
        y = i // 4
        x = i % 4
        total = (pb[y, x, core].astype(F32) + rc[y, x].astype(F32)).astype(BF16)
        sa[y, x // 2, x % 2] = total[:, 0:HALF]
        sb[x, y // 2, y % 2] = total[:, HALF:COLS]
        return carry

    lax.fori_loop(0, 16, core_sum, 0)

    def ring_open(base, me, plus, minus, s, t, u):
        opp, nxt, prv = (me + 2) % 4, (me + 1) % 4, (me + 3) % 4
        plan = (
            (s.at[opp, 0], t.at[0], plus),
            (s.at[opp, 1], t.at[1], minus),
            (s.at[nxt, 1], u.at[0, 1], plus),
            (s.at[prv, 0], u.at[1, 0], minus),
            (s.at[nxt, 0], u.at[0, 0], plus),
            (s.at[prv, 1], u.at[1, 1], minus),
        )
        copies = [
            remote(src, dst, rs_send.at[base + i], rs_recv.at[base + i], dev)
            for i, (src, dst, dev) in enumerate(plan)
        ]
        for copy in copies[:4]:
            copy.start()
        return copies

    def ring_pass(copies, me, s, t):
        nxt, prv = (me + 1) % 4, (me + 3) % 4
        copies[0].wait_recv()
        s[nxt, 0] = (s[nxt, 0].astype(F32) + t[0].astype(F32)).astype(BF16)
        copies[4].start()
        copies[1].wait_recv()
        s[prv, 1] = (s[prv, 1].astype(F32) + t[1].astype(F32)).astype(BF16)
        copies[5].start()

    def ring_close(copies, me, s, u, h):
        return s[me, h].astype(F32) + u[0, h].astype(F32) + u[1, h].astype(F32)

    ca = ring_open(1, yy, yplus, yminus, sa, ta, ua)
    cb = ring_open(7, xx, xplus, xminus, sb, tb, ub)
    ring_pass(ca, yy, sa, ta)
    ring_pass(cb, xx, sb, tb)
    for copies in (ca, cb):
        for i in range(2, 6):
            copies[i].wait_recv()
    for h in range(2):
        total = ring_close(ca, yy, sa, ua, h).astype(BF16)
        for i in range(2):
            for q in range(2):
                sa2[2 * h + i, q] = total[i, :, q * QUART : (q + 1) * QUART]
    for h in range(2):
        total = ring_close(cb, xx, sb, ub, h).astype(BF16)
        for i in range(2):
            for q in range(2):
                sb2[2 * h + i, q] = total[i, :, q * QUART : (q + 1) * QUART]
    ca2 = ring_open(13, xx, xplus, xminus, sa2, ta2, ua2)
    cb2 = ring_open(19, yy, yplus, yminus, sb2, tb2, ub2)
    ring_pass(ca2, xx, sa2, ta2)
    ring_pass(cb2, yy, sb2, tb2)
    for copies in (ca2, cb2):
        for i in range(2, 6):
            copies[i].wait_recv()
    for which, (copies, me, s, u) in enumerate(((ca2, xx, sa2, ua2), (cb2, yy, sb2, ub2))):
        for h in range(2):
            total = ring_close(copies, me, s, u, h)
            for j in range(5):
                for r in range(2):
                    k = ((which * 2 + h) * 5 + j) * 2 + r
                    z1[k // 5, k % 5] = total[
                        8 * r : 8 * r + 8, 128 * j : 128 * j + 128
                    ].astype(BF16)

    seg = z // SEG
    idx = z % SEG

    def in_segment(d):
        i = (idx + d) % SEG
        return i, (g, seg * SEG + i)

    def scatter_step(d, carry):
        i, dev = in_segment(d)
        remote(z1.at[i], r1.at[idx], ar_send.at[0], ar_recv.at[0], dev).start()
        return carry

    lax.fori_loop(1, SEG, scatter_step, 0)
    exchange(3, gs, gr, 8, 16, False)
    r1[idx] = z1[idx]
    seven = r1.at[pl.ds(0, SEG - 1)]
    remote(seven, seven, ar_send.at[0], ar_recv.at[0], partner).wait_recv()
    total = r1[0].astype(F32)
    for i in range(1, SEG):
        total = total + r1[i].astype(F32)
    z2[...] = total.astype(BF16)
    r2[seg] = z2[...]

    def segment_step(d, carry):
        remote(
            z2, r2.at[seg], ar_send.at[1], ar_recv.at[1], (g, (z + SEG * d) % NZ)
        ).start()
        return carry

    lax.fori_loop(1, NSEG, segment_step, 0)
    exchange(3, gs, gr, 16, NZ - 1, False)

    exchange_wait(2, or_, True)
    out_ref[...] = dot(pts[...], rows_of(or_).astype(BF16), 1, 0).astype(BF16)

    three = r2.at[pl.ds(0, NSEG - 1)]
    remote(three, three, ar_send.at[1], ar_recv.at[1], partner).wait_recv()
    total = r2[0].astype(F32)
    for i in range(1, NSEG):
        total = total + r2[i].astype(F32)
    z3[...] = total.astype(BF16)
    r3[idx] = z3[...]

    def share_step(d, carry):
        i, dev = in_segment(d)
        remote(z3, r3.at[idx], ar_send.at[2], ar_recv.at[2], dev).start()
        return carry

    lax.fori_loop(1, SEG, share_step, 0)
    eight = r3.at[pl.ds(0, SEG - 1)]
    last = remote(eight, eight, ar_send.at[2], ar_recv.at[2], partner)
    last.wait_recv()
    for k in range(40):
        j, r = k // 2, k % 2
        tile = r3[k // 5, k % 5].astype(F32)
        if j < 16:
            gu_ref[8 * r : 8 * r + 8, 128 * j : 128 * j + 128] = tile
        else:
            go_ref[8 * r : 8 * r + 8, 128 * (j - 16) : 128 * (j - 15)] = tile

    exchange_wait(3, gr, True)
    grad_ref[...] = dot(pts[...], rows_of(gr).astype(BF16), 1, 0).astype(BF16)

    for which, buf in enumerate((xs, cs, os_, gs)):
        exchange_wait(which, buf, False)
    for copy in (w_x0, w_x1, w_x2, w_x3, w_y0, w_y1, w_y2, w_y3, w_c, p_c):
        copy.wait_send()
    for copies in (ca, cb, ca2, cb2):
        for copy in copies:
            copy.wait_send()
    remote(seven, seven, ar_send.at[0], ar_recv.at[0], partner).wait_send()
    remote(three, three, ar_send.at[1], ar_recv.at[1], partner).wait_send()
    last.wait_send()


def on_device(inputs, cotangent, w_uvqk, w_out, send_perm, recv_perm, lengths, prefixes):
    vmem = pl.BlockSpec(memory_space=pltpu.VMEM)
    smem = pl.BlockSpec(memory_space=pltpu.SMEM)
    blocks = pltpu.VMEM((BLK, BLOCK, D), BF16)

    def buf(*shape, dtype=BF16):
        return pltpu.VMEM(shape, dtype)

    dma = pltpu.SemaphoreType.DMA
    out, grad, gu, go = pl.pallas_call(
        kernel,
        out_shape=(
            jax.ShapeDtypeStruct((ROWS, D), BF16),
            jax.ShapeDtypeStruct((ROWS, D), BF16),
            jax.ShapeDtypeStruct((16, 4 * D), F32),
            jax.ShapeDtypeStruct((16, D), F32),
        ),
        in_specs=[vmem] * 4 + [smem] * 4,
        out_specs=(vmem,) * 4,
        scratch_shapes=[
            *([blocks] * 8),
            buf(4, 4, 2, 16, COLS),
            buf(4, 4, 2, 16, COLS),
            buf(4, 4, 16, COLS),
            buf(4, 2, 2, 16, HALF),
            buf(4, 2, 2, 16, HALF),
            buf(4, 2, 16, QUART),
            buf(4, 2, 16, QUART),
            buf(2, 2, 16, HALF),
            buf(2, 2, 16, HALF),
            buf(2, 16, QUART),
            buf(2, 16, QUART),
            buf(2, 2, 2, 16, HALF),
            buf(2, 2, 2, 16, HALF),
            buf(2, 2, 16, QUART),
            buf(2, 2, 16, QUART),
            buf(SEG, 5, 8, 128),
            buf(SEG, 5, 8, 128),
            buf(5, 8, 128),
            buf(NSEG, 5, 8, 128),
            buf(5, 8, 128),
            buf(SEG, 5, 8, 128),
            buf(ROWS, ROWS),
            buf(ROWS, ROWS),
            buf(ROWS, ROWS, dtype=F32),
            buf(ROWS, D, dtype=F32),
            buf(ROWS, D, dtype=F32),
            buf(ROWS, 128, dtype=F32),
            buf(ROWS, D),
            buf(ROWS, 4 * D),
            buf(ROWS, 4 * D, dtype=F32),
            buf(ROWS, D, dtype=F32),
            buf(ROWS, D),
            buf(ROWS, 4 * D),
            buf(HEADS, ROWS, ROWS),
            buf(HEADS, ROWS, ROWS, dtype=F32),
            dma((4,)),
            dma((4,)),
            dma((9,)),
            dma((9,)),
            dma((25,)),
            dma((25,)),
            dma((3,)),
            dma((3,)),
        ],
        compiler_params=pltpu.CompilerParams(
            collective_id=0, has_side_effects=True, vmem_limit_bytes=60 * 1024 * 1024
        ),
    )(
        inputs[0],
        cotangent[0],
        w_uvqk,
        w_out,
        send_perm[0, 0],
        recv_perm[0, 0],
        lengths[0, 0],
        prefixes[0, 0],
    )
    return (out[None], grad[None], gu, go)


def solution(mesh):
    rows = P("group", "shuf", None)
    return jax.shard_map(
        on_device,
        mesh=mesh,
        in_specs=(rows, rows, P("group", None), P("group", None), rows, rows, rows, rows),
        out_specs=(rows, rows, P("group", None), P("group", None)),
        check_vma=False,
    )
```

time: 714 us -> 146 us (0.20)
  waiting for transfers between devices: 468 us -> 0 us
  Pallas kernels: 0 us -> 141 us
  blocking collectives: 135 us -> 0 us
  starting transfers between devices: 56.3 us -> 0 us
  matrix products: 17.8 us -> 0 us
  between operations: 14.3 us -> 0.65 us
  other arithmetic: 11.6 us -> 0 us
    psum x1 -> x0, waiting for transfers between devices: 258 us -> none  [on_device(): lax.psum(part_proj.astype(jnp.bfloat16), 'shuf').astype(jnp.float32)]
    pallas_call x0 -> x1, Pallas kernels: none -> 141 us  [on_device(): pl.pallas_call(kernel, out_shape=(jax.ShapeDtypeStruct((ROWS, D), BF16),...]
    reduce_scatter x2 -> x0, waiting for transfers between devices: 115 us -> none  [the longest x1 88.9 us: on_device(): lax.psum_scatter(grad_weight.astype(jnp.float32).astype(jnp.bfloat16), 'g...]
    psum x1 -> x0, blocking collectives: 110 us -> none  [on_device(): lax.psum(part_out.astype(jnp.bfloat16), 'shuf').astype(jnp.float32)]
    all_to_all x4 -> x0, waiting for transfers between devices: 94.7 us -> none  [the longest x1 40.8 us: on_device(): lax.all_to_all(outgoing[0], 'shuf', split_axis=0, concat_axis=0, tiled=True)]
    all_to_all x4 -> x0, starting transfers between devices: 56.1 us -> none  [the longest x1 28.7 us: on_device(): lax.all_to_all(outgoing[0], 'shuf', split_axis=0, concat_axis=0, tiled=True)]
    all_gather x1 -> x0, blocking collectives: 24.8 us -> none  [on_device(): lax.all_gather(w_out, 'group', axis=0, tiled=True)]
    dot_general x12 -> x0, matrix products: 17.8 us -> none  [the longest x3 5.25 us: attention(): jnp.einsum('hqk,khd->qhd', weights, values, preferred_element_type=jnp.fl...]
  transfers between devices with their start and end apart: 8 -> 0, of which waited for: 6 -> 0; matrix products, arithmetic and copies ran while one was open for 1% -> 0% of each run, Pallas kernels for 0% -> 0%
where the time goes in v1:
time: 146 us
  Pallas kernels  141 us (97%)
  local copies, waits for them, and re-layouts  4.08 us (3%)
    pallas_call x1, Pallas kernels, on_device(): pl.pallas_call(kernel, out_shape=(jax.ShapeDtypeStruct((ROWS, D), BF16),...  141 us
    unnamed x10, local copies, waits for them, and re-layouts  4.08 us

profile of v1, /device:TPU:6, one launch (start us, length us, event | category | flops | bytes accessed | tf_op | source)
XLA Modules:
  0.0 145.5 jit_solution(12976355486902259944)
XLA Ops:
  0.6 140.8 %shard_map.111 = (bf16[256,512]{1,0:T(8,128)(2,1)}, bf16[256,512]{1,0:T(8,128)(2,1)}, f32[16,2048]{1,0:T(8,128)}, f32[16,512]{1,0:T(8,128)}) custom-call(bf16[256,512]{1,0:T(8,128)(2,1)} %bitcast.8, bf16[256,512]{1,0:T(8,128)(2,1)} %bitcast.9, bf16[16,2048]{1,0:T(8,128)(2,1)} %wu_in.1, bf16[16,512]{1,0:T(8,128)(2,1)} %wo_in.1, s32[32]{0:T(128)} %bitcast.12, ...), custom_call_target="tpu_custom_call" | custom-call | tf_op jit(solution)/shard_map/pallas_call | solution.py:485
  141.4 0.0 copy-start
  141.4 1.7 %copy.16 = bf16[1,256,512]{2,1,0:T(8,128)(2,1)} copy(bf16[1,256,512]{2,1,0:T(8,128)(2,1)} %bitcast.11) | data formatting | bytes 524288
  143.2 0.0 copy-done
  143.2 0.0 copy-start.1
  143.2 0.7 copy.17
  143.9 0.3 copy-done.1
  144.2 0.0 copy-start.2
  144.2 0.7 copy.18
  144.8 0.1 copy-done.2
  144.9 0.6 copy.19
Async XLA Ops:
  141.4 1.7 %copy-start = (bf16[256,512]{1,0:T(8,128)(2,1)S(1)}, bf16[256,512]{1,0:T(8,128)(2,1)}, u32[]{:S(2)}) copy-start(bf16[256,512]{1,0:T(8,128)(2,1)} %get-tuple-element.9) | copy-start | bytes 786436
  143.2 1.0 copy-start.1
  144.2 0.8 copy-start.2

commit v2 on v1

--- a/solution.py
+++ b/solution.py
@@ -16,7 +16,6 @@
 NSEG = 4
 COLS = 2560
 HALF = 1280
-QUART = 640
 EPS = 1e-05
 MESH = pl.DeviceIdType.MESH
 F32 = jnp.float32
@@ -29,12 +28,12 @@
 
 def kernel(
     x_in, c_in, wu_in, wo_in, sp_in, rp_in, len_in, pre_in,
-    out_ref, grad_ref, gu_ref, go_ref,
-    xs, xr, cs, cr, os_, or_, gs, gr,
+    or_, gr, r3,
+    xs, xr, cs, cr, os_, gs,
     wfull, pb, rc, sa, sb, sa2, sb2, ta, tb, ta2, tb2, ua, ub, ua2, ub2,
-    z1, r1, z2, r2, z3, r3,
+    z1, r1, z2, r2, z3,
     pts, ptr, vis, xf, zf, inv, xn, act, dact, mixed, gated, gproj, w8, d8,
-    a2a_send, a2a_recv, ag_send, ag_recv, rs_send, rs_recv, ar_send, ar_recv,
+    meet, a2a_send, a2a_recv, ag_send, ag_recv, rs_send, rs_recv, ar_send, ar_recv,
 ):
     g = lax.axis_index("group")
     z = lax.axis_index("shuf")
@@ -61,13 +60,16 @@
     for dev in (xplus, xminus, yplus, yminus, partner):
         pl.semaphore_signal(barrier, inc=1, device_id=dev, device_id_type=MESH)
 
-    def greet(k, carry):
-        pl.semaphore_signal(
-            barrier, inc=1, device_id=(g, (z + 1 + k) % NZ), device_id_type=MESH
-        )
-        return carry
-
-    lax.fori_loop(0, NZ - 1, greet, 0)
+    def up_down(d):
+        return (g, (z + d) % NZ), (g, (z + NZ - d) % NZ)
+
+    for d in range(1, 5):
+        for dev in up_down(d):
+            pl.semaphore_signal(barrier, inc=1, device_id=dev, device_id_type=MESH)
+
+    def meet_open(i, d):
+        for dev in up_down(d):
+            pl.semaphore_signal(meet.at[i], inc=1, device_id=dev, device_id_type=MESH)
 
     lane = lax.broadcasted_iota(jnp.int32, (1, ROWS), 1)
     row_of = lax.broadcasted_iota(jnp.int32, (ROWS, ROWS), 0)
@@ -78,22 +80,65 @@
             index = index + jnp.where(lane // BLOCK == t, perm_ref[t] * BLOCK, 0)
         return (row_of == index).astype(F32).astype(BF16)
 
-    pts[...] = one_hot(sp_in)
-    ptr[...] = one_hot(rp_in)
-
     def to_blocks(value):
         return value.reshape(BLK, BLOCK, D).astype(BF16)
 
     def rows_of(ref):
         return ref[...].astype(F32).reshape(ROWS, D)
 
+    wfull[yy, xx, core, :, 0 : 4 * D] = wu_in[...]
+    wfull[yy, xx, core, :, 4 * D : COLS] = wo_in[...]
+    pts[...] = one_hot(sp_in)
     xs[...] = to_blocks(dot(pts[...], x_in[...], 0, 0))
     cs[...] = to_blocks(dot(pts[...], c_in[...], 0, 0))
+
+    def exchange(which, src, dst, first, last, far):
+        def step(i, carry):
+            k = NZ - 2 - i if far else i
+            peer = (z + NZ + (k // 2 + 1) * (1 - 2 * (k % 2))) % NZ
+            remote(
+                src.at[peer], dst.at[z], a2a_send.at[which], a2a_recv.at[which], (g, peer)
+            ).start()
+            return carry
+
+        lax.fori_loop(first, last, step, 0)
+
+    def exchange_wait(which, buf, recv):
+        part = buf.at[pl.ds(0, NZ - 1)]
+        copy = remote(
+            part, part, a2a_send.at[which], a2a_recv.at[which], (g, (z + 1) % NZ)
+        )
+        if recv:
+            copy.wait_recv()
+        else:
+            copy.wait_send()
+
+    pl.semaphore_wait(barrier, 5 + 8)
+    meet_open(0, 4)
+    exchange(0, xs, xr, 0, 8, False)
+
+    def gather(i, part, dev):
+        copy = remote(part, part, ag_send.at[i], ag_recv.at[i], dev)
+        copy.start()
+        return copy
+
+    def half_x(x, h):
+        return wfull.at[yy, x, core, :, pl.ds(h * HALF, HALF)]
+
+    def half_y(y, h):
+        return wfull.at[y, pl.ds(2 * h, 2), core]
+
+    own = wfull.at[yy, xx, core]
+    w_x0 = gather(0, own, xplus)
+    w_x1 = gather(1, own, xminus)
+    exchange(1, cs, cr, 0, 8, False)
+    ptr[...] = one_hot(rp_in)
     xr[z] = xs[z]
     cr[z] = cs[z]
-
-    wfull[yy, xx, core, :, 0 : 4 * D] = wu_in[...]
-    wfull[yy, xx, core, :, 4 * D : COLS] = wo_in[...]
+    pl.semaphore_wait(meet.at[0], 2)
+    meet_open(1, 8)
+    exchange(0, xs, xr, 8, 16, False)
+    exchange(1, cs, cr, 8, 16, False)
     ri = lax.broadcasted_iota(jnp.int32, (ROWS, 1), 0)
     uid_r = jnp.zeros((ROWS, 1), jnp.int32)
     uid_k = jnp.zeros((1, ROWS), jnp.int32)
@@ -116,75 +161,28 @@
     )
     vis[...] = allowed * (1.0 / ROWS)
 
-    pl.semaphore_wait(barrier, NZ - 1 + 5)
-
-    def exchange(which, src, dst, first, last, near):
-        def step(k, carry):
-            j = NZ - 2 - k if near else k
-            m = (j + 1) // 2
-            off = NZ // 2 + m * (2 * (j % 2) - 1)
-            peer = (z + off) % NZ
-            remote(
-                src.at[peer], dst.at[z], a2a_send.at[which], a2a_recv.at[which], (g, peer)
-            ).start()
-            return carry
-
-        lax.fori_loop(first, last, step, 0)
-
-    def exchange_wait(which, buf, recv):
-        part = buf.at[pl.ds(0, NZ - 1)]
-        copy = remote(
-            part, part, a2a_send.at[which], a2a_recv.at[which], (g, (z + 1) % NZ)
-        )
-        if recv:
-            copy.wait_recv()
-        else:
-            copy.wait_send()
-
-    exchange(0, xs, xr, 0, NZ - 1, True)
-
-    own = wfull.at[yy, xx, core]
-    w_x0 = remote(own, own, ag_send.at[0], ag_recv.at[0], xplus)
-    w_x1 = remote(own, own, ag_send.at[1], ag_recv.at[1], xminus)
-    w_x0.start()
-    w_x1.start()
-    exchange(1, cs, cr, 0, NZ - 1, False)
-
-    def half_x(x, h):
-        return wfull.at[yy, x, core, :, pl.ds(h * HALF, HALF)]
-
     w_x0.wait_recv()
-    left = half_x((xx + 3) % 4, 0)
-    w_x2 = remote(left, left, ag_send.at[2], ag_recv.at[2], xplus)
-    w_x2.start()
+    w_x2 = gather(2, half_x((xx + 3) % 4, 0), xplus)
     w_x1.wait_recv()
-    right = half_x((xx + 1) % 4, 1)
-    w_x3 = remote(right, right, ag_send.at[3], ag_recv.at[3], xminus)
-    w_x3.start()
+    w_x3 = gather(3, half_x((xx + 1) % 4, 1), xminus)
     w_x2.wait_recv()
     w_x3.wait_recv()
     mine = wfull.at[yy, :, core]
-    w_y0 = remote(mine, mine, ag_send.at[4], ag_recv.at[4], yplus)
-    w_y1 = remote(mine, mine, ag_send.at[5], ag_recv.at[5], yminus)
-    w_y0.start()
-    w_y1.start()
-
-    def half_y(y, h):
-        return wfull.at[y, pl.ds(2 * h, 2), core]
-
+    w_y0 = gather(4, mine, yplus)
+    w_y1 = gather(5, mine, yminus)
+    w_c = [gather(8, mine, partner)]
+    pl.semaphore_wait(meet.at[1], 2)
+    exchange(0, xs, xr, 0, 15, True)
+    exchange(1, cs, cr, 0, 15, True)
     w_y0.wait_recv()
-    down = half_y((yy + 3) % 4, 0)
-    w_y2 = remote(down, down, ag_send.at[6], ag_recv.at[6], yplus)
-    w_y2.start()
+    w_y2 = gather(6, half_y((yy + 3) % 4, 0), yplus)
     w_y1.wait_recv()
-    up = half_y((yy + 1) % 4, 1)
-    w_y3 = remote(up, up, ag_send.at[7], ag_recv.at[7], yminus)
-    w_y3.start()
+    w_y3 = gather(7, half_y((yy + 1) % 4, 1), yminus)
+    w_c.append(gather(9, wfull.at[(yy + 3) % 4, :, core], partner))
+    w_c.append(gather(10, wfull.at[(yy + 1) % 4, :, core], partner))
     w_y2.wait_recv()
     w_y3.wait_recv()
-    column = wfull.at[:, :, core]
-    w_c = remote(column, column, ag_send.at[8], ag_recv.at[8], partner)
-    w_c.start()
+    w_c.append(gather(11, wfull.at[(yy + 2) % 4, :, core], partner))
 
     exchange_wait(0, xr, True)
     x32 = dot(ptr[...], rows_of(xr).astype(BF16), 0, 0)
@@ -196,7 +194,8 @@
     normed_x = centred * scale
     zf[...] = normed_x
     xn[...] = normed_x.astype(BF16)
-    w_c.wait_recv()
+    for copy in w_c:
+        copy.wait_recv()
 
     def weight(c):
         return wfull[:, :, :, :, pl.ds(pl.multiple_of(c * D, D), D)].reshape(D, D)
@@ -248,20 +247,30 @@
     layer = (dot(gated[...], weight(4), 1, 0) + xf[...]).astype(BF16)
     os_[...] = to_blocks(dot(ptr[...], layer, 1, 0))
     or_[z] = os_[z]
-    exchange(2, os_, or_, 0, NZ - 1, False)
+    exchange(2, os_, or_, 0, NZ - 1, True)
 
     exchange_wait(1, cr, True)
     cot = dot(ptr[...], rows_of(cr).astype(BF16), 0, 0)
     cot16 = cot.astype(BF16)
     xf[...] = cot
-    pb[:, :, :, :, 4 * D : COLS] = (
-        dot(gated[...], cot16, 0, 0).astype(BF16).reshape(4, 4, 2, 16, D)
-    )
+    p_c = [
+        remote(pb.at[c, :, :, 1 - core], rc.at[c], rs_send.at[24 + c], rs_recv.at[24 + c], partner)
+        for c in range(5)
+    ]
+    pb[4] = dot(gated[...], cot16, 0, 0).astype(BF16).reshape(4, 4, 2, 16, D)
+    p_c[4].start()
+
+    def weight_grad(c):
+        part = dot(xn[...], gproj[:, c * D : (c + 1) * D], 0, 0)
+        pb[c] = part.astype(BF16).reshape(4, 4, 2, 16, D)
+        p_c[c].start()
+
     g_gated = dot(cot16, weight(4), 1, 1).astype(BF16).astype(F32)
     m_normed = mixed[...]
     g_normed = g_gated * act[:, 0:D].astype(F32)
     g_u = (g_gated * m_normed).astype(BF16).astype(F32)
     gproj[:, 0:D] = (g_u * dact[:, 0:D]).astype(BF16)
+    weight_grad(0)
     g_mixed = m_scale * (
         g_normed
         - jnp.mean(g_normed, axis=-1, keepdims=True)
@@ -291,17 +300,8 @@
 
     lax.fori_loop(0, HEADS // 2, attend_back, 0)
 
-    def weight_grad(c, carry):
-        cols = pl.ds(pl.multiple_of(c * D, D), D)
-        part = dot(xn[...], gproj[:, cols], 0, 0)
-        pb[:, :, :, :, cols] = part.astype(BF16).reshape(4, 4, 2, 16, D)
-        return carry
-
-    lax.fori_loop(0, 4, weight_grad, 0)
-
-    other = pb.at[:, :, 1 - core]
-    p_c = remote(other, rc, rs_send.at[0], rs_recv.at[0], partner)
-    p_c.start()
+    for c in range(1, 4):
+        weight_grad(c)
 
     mixed[...] = dot(gproj[:, 0:D], weight(0), 1, 1)
 
@@ -311,28 +311,20 @@
         return carry
 
     lax.fori_loop(1, 4, input_grad, 0)
-    g_xn = mixed[...]
-    zz = zf[...]
-    g_x = inv[:, 0:1] * (
-        g_xn
-        - jnp.mean(g_xn, axis=-1, keepdims=True)
-        - zz * jnp.mean(g_xn * zz, axis=-1, keepdims=True)
-    ) + xf[...]
-    gs[...] = to_blocks(dot(ptr[...], g_x.astype(BF16), 1, 0))
-    gr[z] = gs[z]
-    exchange(3, gs, gr, 0, 8, False)
-
-    p_c.wait_recv()
-
-    def core_sum(i, carry):
-        y = i // 4
-        x = i % 4
-        total = (pb[y, x, core].astype(F32) + rc[y, x].astype(F32)).astype(BF16)
-        sa[y, x // 2, x % 2] = total[:, 0:HALF]
-        sb[x, y // 2, y % 2] = total[:, HALF:COLS]
-        return carry
-
-    lax.fori_loop(0, 16, core_sum, 0)
+    def core_sum(c):
+        def step(i, carry):
+            y = i // 4
+            x = i % 4
+            total = (pb[c, y, x, core].astype(F32) + rc[c, y, x].astype(F32)).astype(BF16)
+            sa[y, x // 2, x % 2, :, c * D : (c + 1) * D] = total[0:8]
+            sb[x, y // 2, y % 2, :, c * D : (c + 1) * D] = total[8:16]
+            return carry
+
+        lax.fori_loop(0, 16, step, 0)
+
+    for c in (4, 0, 1, 2, 3):
+        p_c[c].wait_recv()
+        core_sum(c)
 
     def ring_open(base, me, plus, minus, s, t, u):
         opp, nxt, prv = (me + 2) % 4, (me + 1) % 4, (me + 3) % 4
@@ -364,8 +356,18 @@
     def ring_close(copies, me, s, u, h):
         return s[me, h].astype(F32) + u[0, h].astype(F32) + u[1, h].astype(F32)
 
-    ca = ring_open(1, yy, yplus, yminus, sa, ta, ua)
-    cb = ring_open(7, xx, xplus, xminus, sb, tb, ub)
+    ca = ring_open(0, yy, yplus, yminus, sa, ta, ua)
+    cb = ring_open(6, xx, xplus, xminus, sb, tb, ub)
+    g_xn = mixed[...]
+    zz = zf[...]
+    g_x = inv[:, 0:1] * (
+        g_xn
+        - jnp.mean(g_xn, axis=-1, keepdims=True)
+        - zz * jnp.mean(g_xn * zz, axis=-1, keepdims=True)
+    ) + xf[...]
+    gs[...] = to_blocks(dot(ptr[...], g_x.astype(BF16), 1, 0))
+    gr[z] = gs[z]
+    exchange(3, gs, gr, 0, 11, True)
     ring_pass(ca, yy, sa, ta)
     ring_pass(cb, xx, sb, tb)
     for copies in (ca, cb):
@@ -375,14 +377,14 @@
         total = ring_close(ca, yy, sa, ua, h).astype(BF16)
         for i in range(2):
             for q in range(2):
-                sa2[2 * h + i, q] = total[i, :, q * QUART : (q + 1) * QUART]
+                sa2[2 * h + i, q] = total[i, :, q * HALF : (q + 1) * HALF]
     for h in range(2):
         total = ring_close(cb, xx, sb, ub, h).astype(BF16)
         for i in range(2):
             for q in range(2):
-                sb2[2 * h + i, q] = total[i, :, q * QUART : (q + 1) * QUART]
-    ca2 = ring_open(13, xx, xplus, xminus, sa2, ta2, ua2)
-    cb2 = ring_open(19, yy, yplus, yminus, sb2, tb2, ub2)
+                sb2[2 * h + i, q] = total[i, :, q * HALF : (q + 1) * HALF]
+    ca2 = ring_open(12, xx, xplus, xminus, sa2, ta2, ua2)
+    cb2 = ring_open(18, yy, yplus, yminus, sb2, tb2, ub2)
     ring_pass(ca2, xx, sa2, ta2)
     ring_pass(cb2, yy, sb2, tb2)
     for copies in (ca2, cb2):
@@ -391,12 +393,9 @@
     for which, (copies, me, s, u) in enumerate(((ca2, xx, sa2, ua2), (cb2, yy, sb2, ub2))):
         for h in range(2):
             total = ring_close(copies, me, s, u, h)
-            for j in range(5):
-                for r in range(2):
-                    k = ((which * 2 + h) * 5 + j) * 2 + r
-                    z1[k // 5, k % 5] = total[
-                        8 * r : 8 * r + 8, 128 * j : 128 * j + 128
-                    ].astype(BF16)
+            for j in range(10):
+                k = (h * 10 + j) * 2 + which
+                z1[k // 5, k % 5] = total[:, 128 * j : 128 * j + 128].astype(BF16)
 
     seg = z // SEG
     idx = z % SEG
@@ -411,7 +410,7 @@
         return carry
 
     lax.fori_loop(1, SEG, scatter_step, 0)
-    exchange(3, gs, gr, 8, 16, False)
+    exchange(3, gs, gr, 11, 17, True)
     r1[idx] = z1[idx]
     seven = r1.at[pl.ds(0, SEG - 1)]
     remote(seven, seven, ar_send.at[0], ar_recv.at[0], partner).wait_recv()
@@ -428,10 +427,7 @@
         return carry
 
     lax.fori_loop(1, NSEG, segment_step, 0)
-    exchange(3, gs, gr, 16, NZ - 1, False)
-
-    exchange_wait(2, or_, True)
-    out_ref[...] = dot(pts[...], rows_of(or_).astype(BF16), 1, 0).astype(BF16)
+    exchange(3, gs, gr, 17, 25, True)
 
     three = r2.at[pl.ds(0, NSEG - 1)]
     remote(three, three, ar_send.at[1], ar_recv.at[1], partner).wait_recv()
@@ -447,23 +443,16 @@
         return carry
 
     lax.fori_loop(1, SEG, share_step, 0)
+    exchange(3, gs, gr, 25, NZ - 1, True)
+    exchange_wait(2, or_, True)
     eight = r3.at[pl.ds(0, SEG - 1)]
     last = remote(eight, eight, ar_send.at[2], ar_recv.at[2], partner)
     last.wait_recv()
-    for k in range(40):
-        j, r = k // 2, k % 2
-        tile = r3[k // 5, k % 5].astype(F32)
-        if j < 16:
-            gu_ref[8 * r : 8 * r + 8, 128 * j : 128 * j + 128] = tile
-        else:
-            go_ref[8 * r : 8 * r + 8, 128 * (j - 16) : 128 * (j - 15)] = tile
-
     exchange_wait(3, gr, True)
-    grad_ref[...] = dot(pts[...], rows_of(gr).astype(BF16), 1, 0).astype(BF16)
 
     for which, buf in enumerate((xs, cs, os_, gs)):
         exchange_wait(which, buf, False)
-    for copy in (w_x0, w_x1, w_x2, w_x3, w_y0, w_y1, w_y2, w_y3, w_c, p_c):
+    for copy in (w_x0, w_x1, w_x2, w_x3, w_y0, w_y1, w_y2, w_y3, *w_c, *p_c):
         copy.wait_send()
     for copies in (ca, cb, ca2, cb2):
         for copy in copies:
@@ -473,6 +462,25 @@
     last.wait_send()
 
 
+def finish(or_ref, gr_ref, sum_ref, sp_in, out_ref, grad_ref, gu_ref, go_ref):
+    lane = lax.broadcasted_iota(jnp.int32, (1, ROWS), 1)
+    index = lane % BLOCK
+    for t in range(BLK):
+        index = index + jnp.where(lane // BLOCK == t, sp_in[t] * BLOCK, 0)
+    hot = lax.broadcasted_iota(jnp.int32, (ROWS, ROWS), 0) == index
+    hot = hot.astype(F32).astype(BF16)
+    for src, dst in ((or_ref, out_ref), (gr_ref, grad_ref)):
+        rows = src[...].astype(F32).reshape(ROWS, D).astype(BF16)
+        dst[...] = dot(hot, rows, 1, 0).astype(BF16)
+    for k in range(40):
+        j, r = k // 2, k % 2
+        tile = sum_ref[k // 5, k % 5].astype(F32)
+        if j < 16:
+            gu_ref[8 * r : 8 * r + 8, 128 * j : 128 * j + 128] = tile
+        else:
+            go_ref[8 * r : 8 * r + 8, 128 * (j - 16) : 128 * (j - 15)] = tile
+
+
 def on_device(inputs, cotangent, w_uvqk, w_out, send_perm, recv_perm, lengths, prefixes):
     vmem = pl.BlockSpec(memory_space=pltpu.VMEM)
     smem = pl.BlockSpec(memory_space=pltpu.SMEM)
@@ -482,39 +490,38 @@
         return pltpu.VMEM(shape, dtype)
 
     dma = pltpu.SemaphoreType.DMA
-    out, grad, gu, go = pl.pallas_call(
+    send_order = send_perm[0, 0]
+    back_out, back_grad, sums = pl.pallas_call(
         kernel,
         out_shape=(
-            jax.ShapeDtypeStruct((ROWS, D), BF16),
-            jax.ShapeDtypeStruct((ROWS, D), BF16),
-            jax.ShapeDtypeStruct((16, 4 * D), F32),
-            jax.ShapeDtypeStruct((16, D), F32),
+            jax.ShapeDtypeStruct((BLK, BLOCK, D), BF16),
+            jax.ShapeDtypeStruct((BLK, BLOCK, D), BF16),
+            jax.ShapeDtypeStruct((SEG, 5, 8, 128), BF16),
         ),
         in_specs=[vmem] * 4 + [smem] * 4,
-        out_specs=(vmem,) * 4,
+        out_specs=(vmem,) * 3,
         scratch_shapes=[
-            *([blocks] * 8),
+            *([blocks] * 6),
             buf(4, 4, 2, 16, COLS),
-            buf(4, 4, 2, 16, COLS),
-            buf(4, 4, 16, COLS),
-            buf(4, 2, 2, 16, HALF),
-            buf(4, 2, 2, 16, HALF),
-            buf(4, 2, 16, QUART),
-            buf(4, 2, 16, QUART),
-            buf(2, 2, 16, HALF),
-            buf(2, 2, 16, HALF),
-            buf(2, 16, QUART),
-            buf(2, 16, QUART),
-            buf(2, 2, 2, 16, HALF),
-            buf(2, 2, 2, 16, HALF),
-            buf(2, 2, 16, QUART),
-            buf(2, 2, 16, QUART),
+            buf(5, 4, 4, 2, 16, D),
+            buf(5, 4, 4, 16, D),
+            buf(4, 2, 2, 8, COLS),
+            buf(4, 2, 2, 8, COLS),
+            buf(4, 2, 8, HALF),
+            buf(4, 2, 8, HALF),
+            buf(2, 2, 8, COLS),
+            buf(2, 2, 8, COLS),
+            buf(2, 8, HALF),
+            buf(2, 8, HALF),
+            buf(2, 2, 2, 8, COLS),
+            buf(2, 2, 2, 8, COLS),
+            buf(2, 2, 8, HALF),
+            buf(2, 2, 8, HALF),
             buf(SEG, 5, 8, 128),
             buf(SEG, 5, 8, 128),
             buf(5, 8, 128),
             buf(NSEG, 5, 8, 128),
             buf(5, 8, 128),
-            buf(SEG, 5, 8, 128),
             buf(ROWS, ROWS),
             buf(ROWS, ROWS),
             buf(ROWS, ROWS, dtype=F32),
@@ -529,12 +536,13 @@
             buf(ROWS, 4 * D),
             buf(HEADS, ROWS, ROWS),
             buf(HEADS, ROWS, ROWS, dtype=F32),
+            pltpu.SemaphoreType.REGULAR((2,)),
             dma((4,)),
             dma((4,)),
-            dma((9,)),
-            dma((9,)),
-            dma((25,)),
-            dma((25,)),
+            dma((12,)),
+            dma((12,)),
+            dma((29,)),
+            dma((29,)),
             dma((3,)),
             dma((3,)),
         ],
@@ -546,11 +554,22 @@
         cotangent[0],
         w_uvqk,
         w_out,
-        send_perm[0, 0],
+        send_order,
         recv_perm[0, 0],
         lengths[0, 0],
         prefixes[0, 0],
     )
+    out, grad, gu, go = pl.pallas_call(
+        finish,
+        out_shape=(
+            jax.ShapeDtypeStruct((ROWS, D), BF16),
+            jax.ShapeDtypeStruct((ROWS, D), BF16),
+            jax.ShapeDtypeStruct((16, 4 * D), F32),
+            jax.ShapeDtypeStruct((16, D), F32),
+        ),
+        in_specs=[vmem] * 3 + [smem],
+        out_specs=(vmem,) * 4,
+    )(back_out, back_grad, sums, send_order)
     return (out[None], grad[None], gu, go)
 
 

time: 146 us -> 140 us (0.959)
  local copies, waits for them, and re-layouts: 4.08 us -> 0 us
  Pallas kernels: 141 us -> 139 us
    unnamed x10 -> x0, local copies, waits for them, and re-layouts: 4.08 us -> none
    pallas_call x1 -> x2, Pallas kernels: 141 us -> 139 us  [the longest x1 137 us: on_device(): pl.pallas_call(kernel, out_shape=(jax.ShapeDtypeStruct((BLK, BLOCK, D), B...]
where the time goes in v2:
time: 140 us
  Pallas kernels  139 us (99%)
    pallas_call x1, Pallas kernels, on_device(): pl.pallas_call(kernel, out_shape=(jax.ShapeDtypeStruct((BLK, BLOCK, D), B...  137 us

profile of v2, /device:TPU:6, one launch (start us, length us, event | category | flops | bytes accessed | tf_op | source)
XLA Modules:
  0.0 139.6 jit_solution(6117751680031146422)
XLA Ops:
  0.6 136.8 %shard_map.111 = (bf16[32,8,512]{2,1,0:T(8,128)(2,1)}, bf16[32,8,512]{2,1,0:T(8,128)(2,1)}, bf16[8,5,8,128]{3,2,1,0:T(8,128)(2,1)}) custom-call(bf16[256,512]{1,0:T(8,128)(2,1)} %bitcast.8, bf16[256,512]{1,0:T(8,128)(2,1)} %bitcast.9, bf16[16,2048]{1,0:T(8,128)(2,1)} %wu_in.1, bf16[16,512]{1,0:T(8,128)(2,1)} %wo_in.1, s32[32]{0:T(128)} %bitcast.10, ...), custom_call_target="tpu_custom_call" | custom-call | tf_op jit(solution)/shard_map/pallas_call | solution.py:494
  137.4 2.2 %shard_map.112 = (bf16[256,512]{1,0:T(8,128)(2,1)}, bf16[256,512]{1,0:T(8,128)(2,1)}, f32[16,2048]{1,0:T(8,128)}, f32[16,512]{1,0:T(8,128)}) custom-call(bf16[32,8,512]{2,1,0:T(8,128)(2,1)} %get-tuple-element.11.or_ref, bf16[32,8,512]{2,1,0:T(8,128)(2,1)} %get-tuple-element.12.gr_ref, bf16[8,5,8,128]{3,2,1,0:T(8,128)(2,1)} %get-tuple-element.13.sum_ref, ...), custom_call_target="tpu_custom_call" | custom-call | tf_op jit(solution)/shard_map/pallas_call | solution.py:562

commit v3 on v2

--- a/solution.py
+++ b/solution.py
@@ -31,7 +31,7 @@
     or_, gr, r3,
     xs, xr, cs, cr, os_, gs,
     wfull, pb, rc, sa, sb, sa2, sb2, ta, tb, ta2, tb2, ua, ub, ua2, ub2,
-    z1, r1, z2, r2, z3,
+    z1, r1, z2, r2, z3, x_buf, c_buf, load_sem,
     pts, ptr, vis, xf, zf, inv, xn, act, dact, mixed, gated, gproj, w8, d8,
     meet, a2a_send, a2a_recv, ag_send, ag_recv, rs_send, rs_recv, ar_send, ar_recv,
 ):
@@ -56,9 +56,25 @@
             device_id=dev, device_id_type=MESH,
         )
 
+    own = wfull.at[yy, xx, core]
+    loads = [
+        pltpu.make_async_copy(src, dst, load_sem.at[i])
+        for i, (src, dst) in enumerate(
+            (
+                (x_in, x_buf),
+                (c_in, c_buf),
+                (wu_in, own.at[:, pl.ds(0, 4 * D)]),
+                (wo_in, own.at[:, pl.ds(4 * D, D)]),
+            )
+        )
+    ]
+
     barrier = pltpu.get_barrier_semaphore()
     for dev in (xplus, xminus, yplus, yminus, partner):
         pl.semaphore_signal(barrier, inc=1, device_id=dev, device_id_type=MESH)
+
+    for copy in loads:
+        copy.start()
 
     def up_down(d):
         return (g, (z + d) % NZ), (g, (z + NZ - d) % NZ)
@@ -86,11 +102,13 @@
     def rows_of(ref):
         return ref[...].astype(F32).reshape(ROWS, D)
 
-    wfull[yy, xx, core, :, 0 : 4 * D] = wu_in[...]
-    wfull[yy, xx, core, :, 4 * D : COLS] = wo_in[...]
     pts[...] = one_hot(sp_in)
-    xs[...] = to_blocks(dot(pts[...], x_in[...], 0, 0))
-    cs[...] = to_blocks(dot(pts[...], c_in[...], 0, 0))
+    loads[0].wait()
+    xs[...] = to_blocks(dot(pts[...], x_buf[...], 0, 0))
+    loads[1].wait()
+    cs[...] = to_blocks(dot(pts[...], c_buf[...], 0, 0))
+    loads[2].wait()
+    loads[3].wait()
 
     def exchange(which, src, dst, first, last, far):
         def step(i, carry):
@@ -128,7 +146,6 @@
     def half_y(y, h):
         return wfull.at[y, pl.ds(2 * h, 2), core]
 
-    own = wfull.at[yy, xx, core]
     w_x0 = gather(0, own, xplus)
     w_x1 = gather(1, own, xminus)
     exchange(1, cs, cr, 0, 8, False)
@@ -397,12 +414,13 @@
                 k = (h * 10 + j) * 2 + which
                 z1[k // 5, k % 5] = total[:, 128 * j : 128 * j + 128].astype(BF16)
 
-    seg = z // SEG
-    idx = z % SEG
+    shift = SEG // 2 * core
+    seg = (z + shift) % NZ // SEG
+    idx = (z + shift) % SEG
 
     def in_segment(d):
         i = (idx + d) % SEG
-        return i, (g, seg * SEG + i)
+        return i, (g, (seg * SEG + i + NZ - shift) % NZ)
 
     def scatter_step(d, carry):
         i, dev = in_segment(d)
@@ -422,7 +440,7 @@
 
     def segment_step(d, carry):
         remote(
-            z2, r2.at[seg], ar_send.at[1], ar_recv.at[1], (g, (z + SEG * d) % NZ)
+            z2, r2.at[seg], ar_send.at[1], ar_recv.at[1], (g, (z + SEG * (d % 3 + 1)) % NZ)
         ).start()
         return carry
 
@@ -498,7 +516,7 @@
             jax.ShapeDtypeStruct((BLK, BLOCK, D), BF16),
             jax.ShapeDtypeStruct((SEG, 5, 8, 128), BF16),
         ),
-        in_specs=[vmem] * 4 + [smem] * 4,
+        in_specs=[pl.BlockSpec(memory_space=pl.ANY)] * 4 + [smem] * 4,
         out_specs=(vmem,) * 3,
         scratch_shapes=[
             *([blocks] * 6),
@@ -522,6 +540,9 @@
             buf(5, 8, 128),
             buf(NSEG, 5, 8, 128),
             buf(5, 8, 128),
+            buf(ROWS, D),
+            buf(ROWS, D),
+            dma((4,)),
             buf(ROWS, ROWS),
             buf(ROWS, ROWS),
             buf(ROWS, ROWS, dtype=F32),

time: 140 us -> 139 us (level); the launches traced: 140 us -> 137 us
  Pallas kernels: 139 us -> 136 us
    pallas_call x1, Pallas kernels: 137 us -> 134 us  [on_device(): pl.pallas_call(kernel, out_shape=(jax.ShapeDtypeStruct((BLK, BLOCK, D), B...]
where the time goes in v3:
time: 139 us; the launch traced here: 137 us
  Pallas kernels  136 us (98%)
    pallas_call x1, Pallas kernels, on_device(): pl.pallas_call(kernel, out_shape=(jax.ShapeDtypeStruct((BLK, BLOCK, D), B...  134 us

profile of v3, /device:TPU:6, one launch (start us, length us, event | category | flops | bytes accessed | tf_op | source)
XLA Modules:
  0.0 136.8 jit_solution(15321176677697984373)
XLA Ops:
  0.6 134.0 %shard_map.111 = (bf16[32,8,512]{2,1,0:T(8,128)(2,1)}, bf16[32,8,512]{2,1,0:T(8,128)(2,1)}, bf16[8,5,8,128]{3,2,1,0:T(8,128)(2,1)}) custom-call(bf16[256,512]{1,0:T(8,128)(2,1)} %bitcast.8, bf16[256,512]{1,0:T(8,128)(2,1)} %bitcast.9, bf16[16,2048]{1,0:T(8,128)(2,1)} %wu_in.1, bf16[16,512]{1,0:T(8,128)(2,1)} %wo_in.1, s32[32]{0:T(128)} %bitcast.10, ...), custom_call_target="tpu_custom_call" | custom-call | tf_op jit(solution)/shard_map/pallas_call | solution.py:512
  134.6 2.2 %shard_map.112 = (bf16[256,512]{1,0:T(8,128)(2,1)}, bf16[256,512]{1,0:T(8,128)(2,1)}, f32[16,2048]{1,0:T(8,128)}, f32[16,512]{1,0:T(8,128)}) custom-call(bf16[32,8,512]{2,1,0:T(8,128)(2,1)} %get-tuple-element.11.or_ref, bf16[32,8,512]{2,1,0:T(8,128)(2,1)} %get-tuple-element.12.gr_ref, bf16[8,5,8,128]{3,2,1,0:T(8,128)(2,1)} %get-tuple-element.13.sum_ref, ...), custom_call_target="tpu_custom_call" | custom-call | tf_op jit(solution)/shard_map/pallas_call | solution.py:583
